TPU v7x, 32 devices: a whole 2x2x4 slice. The times are simulated.
32 devices in a mesh: boson: 8 (over z, x), block: 4 (over y, core).
Axes of the slice: x: 2, y: 2, z: 4, core: 2. Of those that a mesh axis runs over, the one named last changes fastest.
Arguments:
- gamma_ph: bfloat16 [32, 1024, 1024], P('boson', 'block'), may hold values from -6 to 6
- full_ph: bfloat16 [32, 1024, 1024], P('boson', 'block'), may hold values from -0.1875 to 0.1875
- chi_ph: float32 [32, 1024], P('boson'), may hold values from 0.3 to 3
- pp_vertex: bfloat16 [32, 1024, 1024], P('boson', 'block'), may hold values from -0.1875 to 0.1875
- chi_pp: float32 [32, 1024], P('boson'), may hold values from 0.3 to 3
- relabel: int32 [32, 16, 8], replicated, may hold values from 0 to 31, as said below
Outputs:
- vertex_new: bfloat16 [32, 1024, 1024], P('boson', 'block')
Inputs may be any that keep to these rules, and one draw needn't show every extreme that they name: `relabel`: for each row tile and column block the table is a permutation of the 32 points. The owner of the target point (target // 4) is the source's owner (q // 4) plus a shift modulo 8, and both this shift and the target's position among its owner's points (target % 4) depend only on the row tile, the column block and q % 4. Row tiles b * 4 to (b + 1) * 4 - 1 form row block b; within one row block, at most 17 of the 128 triples of position, row tile and column block share a shift, and some shift is shared by exactly 17; in every row block the shifts 1, 4 and 7 each occur.
All inputs are finite; a program needn't handle non-finite values.
Results may differ from a plain program's by a relative error of at most 0.0063.
Values may be sent and summed in bfloat16 or wider, within the bound.
A program may use at most 128 MiB of HBM per device.

v0:
```python
import jax
import jax.numpy as jnp
from jax import lax
from jax.sharding import PartitionSpec as P

CB = 8
RS = 4


def to_tiles(matrix):
    points, row_count, order_size = matrix.shape
    tile_width = order_size // CB
    tile_rows = row_count // RS
    return (
        matrix.reshape(points, RS, tile_rows, CB, tile_width)
        .transpose(0, 1, 3, 2, 4)
        .reshape(points * RS * CB, tile_rows, tile_width)
    )


def from_tiles(tile_stack, points):
    total_tiles, tile_rows, tile_width = tile_stack.shape
    return (
        tile_stack.reshape(points, RS, CB, tile_rows, tile_width)
        .transpose(0, 1, 3, 2, 4)
        .reshape(points, RS * tile_rows, CB * tile_width)
    )


def scale_columns(left_side, column_scale):
    return (left_side.astype(jnp.float32) * column_scale[:, None, :]).astype(jnp.bfloat16)


def product_adder(scaled, shard_piece):
    return jnp.einsum("qij,qjk->qik", scaled, shard_piece, preferred_element_type=jnp.float32)


def pack_slots(tile_stack, slot_of_item, slot_total):
    item_total = tile_stack.shape[0]
    matches = (slot_of_item[None, :] == jnp.arange(slot_total, dtype=jnp.int32)[:, None]).astype(
        jnp.int32
    )
    item_index = jnp.sum(matches * jnp.arange(item_total, dtype=jnp.int32)[None, :], axis=1)
    filled = jnp.sum(matches, axis=1).astype(tile_stack.dtype)
    return jnp.take(tile_stack, item_index, axis=0) * filled[:, None, None]


def local(gamma_ph, full_ph, chi_ph, pp_vertex, chi_pp, relabel):
    points = gamma_ph.shape[0]
    nboson = lax.axis_size("boson")
    boson_here = lax.axis_index("boson")
    block_here = lax.axis_index("block")
    item_total = points * RS * CB
    capacity = -(-item_total // nboson) + 1
    phi_ph = product_adder(
        scale_columns(gamma_ph, chi_ph), lax.all_gather(full_ph, "block", axis=1, tiled=True)
    )
    ph_tiles = to_tiles(phi_ph.astype(jnp.bfloat16))
    tile_shape = ph_tiles.shape[1:]
    own_targets = lax.dynamic_slice(
        relabel, (boson_here * points, block_here * RS, 0), (points, RS, CB)
    ).reshape(item_total)
    shifts = (own_targets // points - boson_here) % nboson
    item_range = jnp.arange(item_total, dtype=jnp.int32)
    target = own_targets % points * (RS * CB) + item_range % (RS * CB)
    gather_order = jnp.sum(
        (target[None, :] == item_range[:, None]).astype(jnp.int32) * item_range[None, :], axis=1
    )
    earlier = (shifts[None, :] == shifts[:, None]) & (item_range[None, :] < item_range[:, None])
    slot_rank = jnp.sum(earlier.astype(jnp.int32), axis=1)
    send_slot = (boson_here + shifts) % nboson * capacity + slot_rank
    recv_slot = (boson_here - shifts) % nboson * capacity + slot_rank
    outgoing = pack_slots(ph_tiles, send_slot, nboson * capacity).reshape(
        (nboson, capacity) + tile_shape
    )
    incoming = lax.all_to_all(outgoing, "boson", split_axis=0, concat_axis=0, tiled=True).reshape(
        (nboson * capacity,) + tile_shape
    )
    arrived = jnp.take(incoming, recv_slot, axis=0)
    relabelled = from_tiles(jnp.take(arrived, gather_order, axis=0), points)
    phi_pp = product_adder(
        scale_columns(relabelled, chi_pp), lax.all_gather(pp_vertex, "block", axis=1, tiled=True)
    ).astype(jnp.bfloat16)
    leaving = jnp.take(to_tiles(phi_pp), target, axis=0)
    outgoing_back = pack_slots(leaving, recv_slot, nboson * capacity).reshape(
        (nboson, capacity) + tile_shape
    )
    incoming_back = lax.all_to_all(
        outgoing_back, "boson", split_axis=0, concat_axis=0, tiled=True
    ).reshape((nboson * capacity,) + tile_shape)
    returned = jnp.take(incoming_back, send_slot, axis=0)
    output = (
        gamma_ph.astype(jnp.float32) + phi_ph + from_tiles(returned, points).astype(jnp.float32)
    )
    return output.astype(jnp.bfloat16)


def solution(mesh):
    placed = (
        P("boson", "block", None),
        P("boson", "block", None),
        P("boson", None),
        P("boson", "block", None),
        P("boson", None),
        P(),
    )
    return jax.shard_map(
        local, mesh=mesh, in_specs=placed, out_specs=P("boson", "block", None), check_vma=False
    )
```

profile of v0, /device:TPU:0, one launch (start us, length us, event | category | flops | bytes accessed | tf_op | source)
XLA Modules:
  0.0 260.7 jit_solution(9437787763903134914)
XLA Ops:
  6.5 0.7 all-gather.3.cloned.1.call-update
  7.3 0.7 all-gather.5.cloned.1.call-update
  8.8 61.1 %all-gather.3.cloned.1.call-done = bf16[4,1024,1024]{2,1,0:T(8,128)(2,1)} async-done(((bf16[4,256,1024]{2,1,0:T(8,128)(2,1)}), bf16[4,1024,1024]{2,1,0:T(8,128)(2,1)}) %all-gather.3.cloned.1.call-update) | async-done | bytes 8388624 | tf_op jit(solution)/shard_map/all_gather | solution.py:56
  69.9 7.7 %fusion.22 = (bf16[4,256,1024]{2,1,0:T(8,128)(2,1)S(1)}, f32[4,256,1024]{2,1,0:T(8,128)}) fusion(bf16[4,1024,1024]{2,1,0:T(8,128)(2,1)} %all-gather.3.cloned.1.call-done, bf16[4,256,1024]{2,1,0:T(8,128)(2,1)S(1)} %copy-done.2, f32[4,1024]{1,0:T(4,128)S(1)} %copy-done.4), kind=kOutput, calls=%fused_computation.79 | convolution fusion | flops 2151677952 | bytes 16793600 | tf_op jit(solution)/shard_map/qij,qjk->qik/dot_general | solution.py:35
  77.6 0.6 copy.22
  78.2 0.6 copy.18
  78.8 2.4 gather_fusion
  81.3 3.5 %select_multiply_fusion.1 = bf16[136,64,128]{2,1,0:T(8,128)(2,1)} fusion(bf16[136,64,128]{2,1,0:T(8,128)(2,1)} %gather_fusion, pred[136]{0:T(512)(128)(4,1)S(1)} %compare_and_fusion.5, bf16[136]{0:T(256)(128)(2,1)S(1)} %convert_element_type.72), kind=kLoop, calls=%fused_computation.15 | loop fusion | flops 2228224 | bytes 4456856 | tf_op jit(solution)/shard_map/mul | solution.py:45
  84.8 5.3 %all-to-all-start = ((bf16[8,17,64,128]{3,2,1,0:T(8,128)(2,1)}), bf16[8,17,64,128]{3,2,1,0:T(8,128)(2,1)S(1)}, u32[]{:S(2)}, u32[]{:S(2)}) async-start(bf16[8,17,64,128]{3,2,1,0:T(8,128)(2,1)} %bitcast.2), calls=%async_computation | async-start | bytes 4456448 | tf_op jit(solution)/shard_map/all_to_all | solution.py:76
  90.3 51.2 %all-to-all-done = bf16[8,17,64,128]{3,2,1,0:T(8,128)(2,1)S(1)} async-done(((bf16[8,17,64,128]{3,2,1,0:T(8,128)(2,1)}), bf16[8,17,64,128]{3,2,1,0:T(8,128)(2,1)S(1)}, u32[]{:S(2)}, u32[]{:S(2)}) %all-to-all-start) | async-done | bytes 2228256 | tf_op jit(solution)/shard_map/all_to_all | solution.py:76
  141.6 2.1 gather_fusion.1
  143.7 1.9 broadcast_select_fusion.3
  145.6 2.1 gather_fusion.2
  147.7 1.9 broadcast_select_fusion.2
  149.6 0.5 convert_bitcast_fusion.1
  150.1 5.2 %copy.19 = f32[4,4,64,8,128]{4,3,2,1,0:T(8,128)} copy(f32[4,4,64,8,128]{4,2,3,1,0:T(8,128)S(1)} %convert_bitcast_fusion.1) | data formatting | bytes 8388608 | tf_op jit(solution)/shard_map/convert_element_type | solution.py:31
  155.3 4.9 %reshape.233 = f32[4,256,1024]{2,1,0:T(8,128)} reshape(f32[4,4,64,8,128]{4,3,2,1,0:T(8,128)} %copy.19) | data formatting | bytes 8388608 | tf_op jit(solution)/shard_map/convert_element_type | solution.py:31
  160.2 7.0 %fusion.8 = bf16[4,256,1024]{2,1,0:T(8,128)(2,1)S(1)} fusion(bf16[4,1024,1024]{2,1,0:T(8,128)(2,1)} %all-gather.5.cloned.1.call-done, f32[4,256,1024]{2,1,0:T(8,128)} %reshape.233, f32[4,1024]{1,0:T(4,128)S(1)} %copy-done.5), kind=kOutput, calls=%fused_computation.24 | convolution fusion | flops 2150629376 | bytes 14696448 | tf_op jit(solution)/shard_map/qij,qjk->qik/dot_general | solution.py:35
  167.2 0.6 copy.23
  167.8 0.6 copy.20
  168.4 2.1 gather_fusion.3
  170.6 1.9 broadcast_select_fusion.1
  172.4 2.4 gather_fusion.4
  174.8 3.2 %select_multiply_fusion = bf16[136,64,128]{2,1,0:T(8,128)(2,1)} fusion(bf16[136,64,128]{2,1,0:T(8,128)(2,1)} %gather_fusion.4, pred[136]{0:T(512)(128)(4,1)S(1)} %compare_and_fusion.1, bf16[136]{0:T(256)(128)(2,1)S(1)} %convert_element_type.80), kind=kLoop, calls=%fused_computation.14 | loop fusion | flops 2228224 | bytes 4456856 | tf_op jit(solution)/shard_map/mul | solution.py:45
  178.0 3.8 %all-to-all-start.1 = ((bf16[8,17,64,128]{3,2,1,0:T(8,128)(2,1)}), bf16[8,17,64,128]{3,2,1,0:T(8,128)(2,1)S(1)}, u32[]{:S(2)}, u32[]{:S(2)}) async-start(bf16[8,17,64,128]{3,2,1,0:T(8,128)(2,1)} %bitcast.8), calls=%async_computation.1 | async-start | bytes 4456448 | tf_op jit(solution)/shard_map/all_to_all | solution.py:88
  181.9 51.1 %all-to-all-done.1 = bf16[8,17,64,128]{3,2,1,0:T(8,128)(2,1)S(1)} async-done(((bf16[8,17,64,128]{3,2,1,0:T(8,128)(2,1)}), bf16[8,17,64,128]{3,2,1,0:T(8,128)(2,1)S(1)}, u32[]{:S(2)}, u32[]{:S(2)}) %all-to-all-start.1) | async-done | bytes 2228256 | tf_op jit(solution)/shard_map/all_to_all | solution.py:88
  233.0 2.1 gather_fusion.5
  235.1 1.9 broadcast_select_fusion
  237.0 0.5 convert_bitcast_fusion
  237.4 5.3 %copy.21 = f32[4,4,64,8,128]{4,3,2,1,0:T(8,128)} copy(f32[4,4,64,8,128]{4,2,3,1,0:T(8,128)S(1)} %convert_bitcast_fusion) | data formatting | bytes 8388608 | tf_op jit(solution)/shard_map/convert_element_type | solution.py:93
  242.7 5.0 %reshape.234 = f32[4,256,1024]{2,1,0:T(8,128)} reshape(f32[4,4,64,8,128]{4,3,2,1,0:T(8,128)} %copy.21) | data formatting | bytes 8388608 | tf_op jit(solution)/shard_map/convert_element_type | solution.py:93
  247.7 6.1 %fusion.2 = bf16[4,256,1024]{2,1,0:T(8,128)(2,1)} fusion(f32[4,256,1024]{2,1,0:T(8,128)} %reshape.234, f32[4,256,1024]{2,1,0:T(8,128)} %get-tuple-element.21, bf16[4,256,1024]{2,1,0:T(8,128)(2,1)S(1)} %copy-done.3), kind=kLoop, calls=%fused_computation.10 | loop fusion | flops 4194304 | bytes 12582912 | tf_op jit(solution)/shard_map/convert_element_type | solution.py:95
  (41 shorter events, 1.0 us)
Async XLA Ops:
  6.5 1.5 copy-start
  6.5 63.4 %copy-start.2 = (bf16[4,256,1024]{2,1,0:T(8,128)(2,1)S(1)}, bf16[4,256,1024]{2,1,0:T(8,128)(2,1)}, u32[]{:S(2)}) copy-start(bf16[4,256,1024]{2,1,0:T(8,128)(2,1)} %param.12) | copy-start | bytes 6291460
  6.5 63.4 %copy-start.4 = (f32[4,1024]{1,0:T(4,128)S(1)}, f32[4,1024]{1,0:T(4,128)}, u32[]{:S(2)}) copy-start(f32[4,1024]{1,0:T(4,128)} %param.14) | copy-start | bytes 49156
  6.5 63.4 %all-gather.3.cloned.1.call-start = ((), (), s32[]{:S(2)}) async-start(), calls=%async_computation.2 | async-start | bytes 10485760 | tf_op jit(solution)/shard_map/all_gather | solution.py:56
  7.3 152.9 %all-gather.5.cloned.1.call-start = ((), (), s32[]{:S(2)}) async-start(), calls=%async_computation.3 | async-start | bytes 10485760 | tf_op jit(solution)/shard_map/all_gather | solution.py:82
  84.8 56.8 %all-to-all-start = ((bf16[8,17,64,128]{3,2,1,0:T(8,128)(2,1)}), bf16[8,17,64,128]{3,2,1,0:T(8,128)(2,1)S(1)}, u32[]{:S(2)}, u32[]{:S(2)}) async-start(bf16[8,17,64,128]{3,2,1,0:T(8,128)(2,1)} %bitcast.2), calls=%async_computation | async-start | bytes 4456448 | tf_op jit(solution)/shard_map/all_to_all | solution.py:76
  155.3 4.9 %copy-start.5 = (f32[4,1024]{1,0:T(4,128)S(1)}, f32[4,1024]{1,0:T(4,128)}, u32[]{:S(2)}) copy-start(f32[4,1024]{1,0:T(4,128)} %param.16) | copy-start | bytes 49156
  178.0 54.9 %all-to-all-start.1 = ((bf16[8,17,64,128]{3,2,1,0:T(8,128)(2,1)}), bf16[8,17,64,128]{3,2,1,0:T(8,128)(2,1)S(1)}, u32[]{:S(2)}, u32[]{:S(2)}) async-start(bf16[8,17,64,128]{3,2,1,0:T(8,128)(2,1)} %bitcast.8), calls=%async_computation.1 | async-start | bytes 4456448 | tf_op jit(solution)/shard_map/all_to_all | solution.py:88
  242.7 5.0 %copy-start.3 = (bf16[4,256,1024]{2,1,0:T(8,128)(2,1)S(1)}, bf16[4,256,1024]{2,1,0:T(8,128)(2,1)}, u32[]{:S(2)}) copy-start(bf16[4,256,1024]{2,1,0:T(8,128)(2,1)} %param.12) | copy-start | bytes 6291460
  247.7 6.1 %copy-start.1 = (s32[32,16,8]{0,2,1:T(8,128)S(1)}, s32[32,16,8]{0,2,1:T(8,128)}, u32[]{:S(2)}) copy-start(s32[32,16,8]{0,2,1:T(8,128)} %param.17) | copy-start | bytes 49156
Sparse Core Ops, SparseCore 0:
  8.9 60.9 all-gather.2
  71.5 58.2 all-gather.4
where the time goes:
time: 261 us
  waiting for transfers between devices  165 us (63%)
  local copies, waits for them, and re-layouts  36.5 us (14%)
  other arithmetic  21.8 us (8%)
  matrix products  14.7 us (6%)
  between operations  13.7 us (5%)
  starting transfers between devices  9.13 us (3%)
    all_gather x1, waiting for transfers between devices, local(): lax.all_gather(full_ph, 'block', axis=1, tiled=True)  61.1 us
    all_to_all x1, waiting for transfers between devices, local(): lax.all_to_all(outgoing, 'boson', split_axis=0, concat_axis=0, tiled=True)  51.2 us
    all_to_all x1, waiting for transfers between devices, local(): lax.all_to_all(outgoing_back, 'boson', split_axis=0, concat_axis=0, tiled...  51.1 us
    dot_general x2, matrix products, product_adder(): jnp.einsum('qij,qjk->qik', scaled, shard_piece, preferred_element_type=jn...  14.7 us
    convert_element_type x2, local copies, waits for them, and re-layouts, local(): from_tiles(returned, points).astype(jnp.float32)  10.3 us
    convert_element_type x2, local copies, waits for them, and re-layouts, scale_columns(): left_side.astype(jnp.float32) * column_scale[:, None, :]  10.1 us
    mul x2, other arithmetic, pack_slots(): return jnp.take(tile_stack, item_index, axis=0) * filled[:, None, None]  6.72 us
    convert_element_type x1, other arithmetic, local(): return output.astype(jnp.bfloat16)  6.07 us
  transfers between devices with their start and end apart: 4, of which 3 were waited for; matrix products, arithmetic and copies ran while one was open for 13% of the time, Pallas kernels for 0%

commit v1 on v0

--- a/solution.py
+++ b/solution.py
@@ -53,7 +53,13 @@
     item_total = points * RS * CB
     capacity = -(-item_total // nboson) + 1
     phi_ph = product_adder(
-        scale_columns(gamma_ph, chi_ph), lax.all_gather(full_ph, "block", axis=1, tiled=True)
+        scale_columns(gamma_ph, chi_ph),
+        jnp.concatenate(
+            lax.all_to_all(
+                jnp.stack(lax.axis_size("block") * [full_ph]), "block", split_axis=0, concat_axis=0
+            ),
+            1,
+        ),
     )
     ph_tiles = to_tiles(phi_ph.astype(jnp.bfloat16))
     tile_shape = ph_tiles.shape[1:]

time: 261 us -> 357 us (1.37)
  waiting for transfers between devices: 165 us -> 241 us
  local copies, waits for them, and re-layouts: 36.5 us -> 49.9 us
  starting transfers between devices: 9.13 us -> 16.1 us
    all_to_all x0 -> x1, waiting for transfers between devices: none -> 138 us  [local(): lax.all_to_all(jnp.stack(lax.axis_size('block') * [full_ph]), 'block', sp...]
    all_gather x1 -> x0, waiting for transfers between devices: 61.1 us -> none  [local(): lax.all_gather(full_ph, 'block', axis=1, tiled=True)]
    reshape x0 -> x1, local copies, waits for them, and re-layouts: none -> 8.1 us  [local(): jnp.concatenate(lax.all_to_all(jnp.stack(lax.axis_size('block') * [full_p...]
    all_to_all x0 -> x1, starting transfers between devices: none -> 5.67 us  [local(): lax.all_to_all(jnp.stack(lax.axis_size('block') * [full_ph]), 'block', sp...]
    another operation x0 -> x1, local copies, waits for them, and re-layouts: none -> 4.37 us  [local(): jnp.stack(lax.axis_size('block') * [full_ph])]
where the time goes in v1:
time: 357 us; the launch traced here: 356 us
  waiting for transfers between devices  241 us (68%)
  local copies, waits for them, and re-layouts  49.9 us (14%)
  other arithmetic  21.5 us (6%)
  starting transfers between devices  16.1 us (5%)
  matrix products  14.7 us (4%)
  between operations  13.7 us (4%)
    all_to_all x1, waiting for transfers between devices, local(): lax.all_to_all(jnp.stack(lax.axis_size('block') * [full_ph]), 'block', sp...  138 us
    all_to_all x1, waiting for transfers between devices, local(): lax.all_to_all(outgoing_back, 'boson', split_axis=0, concat_axis=0, tiled...  51.1 us
    all_to_all x1, waiting for transfers between devices, local(): lax.all_to_all(outgoing, 'boson', split_axis=0, concat_axis=0, tiled=True)  50.9 us
    dot_general x2, matrix products, product_adder(): jnp.einsum('qij,qjk->qik', scaled, shard_piece, preferred_element_type=jn...  14.7 us
    convert_element_type x2, local copies, waits for them, and re-layouts, local(): from_tiles(returned, points).astype(jnp.float32)  10.3 us
    convert_element_type x2, local copies, waits for them, and re-layouts, scale_columns(): left_side.astype(jnp.float32) * column_scale[:, None, :]  10.1 us
    reshape x1, local copies, waits for them, and re-layouts, local(): jnp.concatenate(lax.all_to_all(jnp.stack(lax.axis_size('block') * [full_p...  8.1 us
  transfers between devices with their start and end apart: 4, of which 3 were waited for; matrix products, arithmetic and copies ran while one was open for 13% of the time, Pallas kernels for 0%

profile of v1, /device:TPU:0, one launch (start us, length us, event | category | flops | bytes accessed | tf_op | source)
XLA Modules:
  0.0 356.4 jit_solution(3400193529500774403)
XLA Ops:
  6.5 0.7 all-gather.2.cloned.1.call-update
  7.3 0.9 copy-done.4
  8.2 4.4 %stack.2 = bf16[4,4,256,1024]{3,2,1,0:T(8,128)(2,1)} broadcast(bf16[4,256,1024]{2,1,0:T(8,128)(2,1)S(1)} %copy-done.4), dimensions={1,2,3} | broadcast | bytes 10485760 | tf_op jit(solution)/shard_map/stack | solution.py:59
  12.5 5.7 %all-to-all-start = ((bf16[4,4,256,1024]{3,2,1,0:T(8,128)(2,1)}), bf16[4,4,256,1024]{3,2,1,0:T(8,128)(2,1)}, u32[]{:S(2)}, u32[]{:S(2)}) async-start(bf16[4,4,256,1024]{3,2,1,0:T(8,128)(2,1)} %stack.2), calls=%async_computation | async-start | bytes 16777216 | tf_op jit(solution)/shard_map/all_to_all | solution.py:58
  19.0 137.9 %all-to-all-done = bf16[4,4,256,1024]{3,2,1,0:T(8,128)(2,1)} async-done(((bf16[4,4,256,1024]{3,2,1,0:T(8,128)(2,1)}), bf16[4,4,256,1024]{3,2,1,0:T(8,128)(2,1)}, u32[]{:S(2)}, u32[]{:S(2)}) %all-to-all-start) | async-done | bytes 8388640 | tf_op jit(solution)/shard_map/all_to_all | solution.py:58
  156.9 8.1 %copy.23 = bf16[4,4,256,1024]{3,2,1,0:T(8,128)(2,1)} copy(bf16[4,4,256,1024]{3,2,0,1:T(8,128)(2,1)} %bitcast) | data formatting | bytes 16777216 | tf_op jit(solution)/shard_map/reshape | solution.py:57
  165.0 7.7 %fusion.22 = (bf16[4,256,1024]{2,1,0:T(8,128)(2,1)S(1)}, f32[4,256,1024]{2,1,0:T(8,128)}) fusion(bf16[4,1024,1024]{2,1,0:T(8,128)(2,1)} %bitcast.34, bf16[4,256,1024]{2,1,0:T(8,128)(2,1)S(1)} %copy-done.2, f32[4,1024]{1,0:T(4,128)S(1)} %copy-done.5), kind=kOutput, calls=%fused_computation.79 | convolution fusion | flops 2151677952 | bytes 16793600 | tf_op jit(solution)/shard_map/qij,qjk->qik/dot_general | solution.py:35
  172.7 0.6 copy.29
  174.0 2.4 gather_fusion
  176.4 3.2 select_multiply_fusion.1
  179.6 6.6 %all-to-all-start.1 = ((bf16[8,17,64,128]{3,2,1,0:T(8,128)(2,1)}), bf16[8,17,64,128]{3,2,1,0:T(8,128)(2,1)S(1)}, u32[]{:S(2)}, u32[]{:S(2)}) async-start(bf16[8,17,64,128]{3,2,1,0:T(8,128)(2,1)} %bitcast.4), calls=%async_computation.1 | async-start | bytes 4456448 | tf_op jit(solution)/shard_map/all_to_all | solution.py:82
  186.5 50.9 %all-to-all-done.1 = bf16[8,17,64,128]{3,2,1,0:T(8,128)(2,1)S(1)} async-done(((bf16[8,17,64,128]{3,2,1,0:T(8,128)(2,1)}), bf16[8,17,64,128]{3,2,1,0:T(8,128)(2,1)S(1)}, u32[]{:S(2)}, u32[]{:S(2)}) %all-to-all-start.1) | async-done | bytes 2228256 | tf_op jit(solution)/shard_map/all_to_all | solution.py:82
  237.3 2.1 gather_fusion.1
  239.5 1.9 broadcast_select_fusion.3
  241.3 2.1 gather_fusion.2
  243.5 1.9 broadcast_select_fusion.2
  245.8 5.2 %copy.26 = f32[4,4,64,8,128]{4,3,2,1,0:T(8,128)} copy(f32[4,4,64,8,128]{4,2,3,1,0:T(8,128)S(1)} %convert_bitcast_fusion.1) | data formatting | bytes 8388608 | tf_op jit(solution)/shard_map/convert_element_type | solution.py:31
  251.0 4.9 %reshape.243 = f32[4,256,1024]{2,1,0:T(8,128)} reshape(f32[4,4,64,8,128]{4,3,2,1,0:T(8,128)} %copy.26) | data formatting | bytes 8388608 | tf_op jit(solution)/shard_map/convert_element_type | solution.py:31
  255.9 7.0 %fusion.8 = bf16[4,256,1024]{2,1,0:T(8,128)(2,1)S(1)} fusion(bf16[4,1024,1024]{2,1,0:T(8,128)(2,1)} %all-gather.2.cloned.1.call-done, f32[4,256,1024]{2,1,0:T(8,128)} %reshape.243, f32[4,1024]{1,0:T(4,128)S(1)} %copy-done.6), kind=kOutput, calls=%fused_computation.24 | convolution fusion | flops 2150629376 | bytes 14696448 | tf_op jit(solution)/shard_map/qij,qjk->qik/dot_general | solution.py:35
  262.9 0.6 copy.30
  263.6 0.6 copy.27
  264.2 2.1 gather_fusion.3
  266.3 1.9 broadcast_select_fusion.1
  268.2 2.4 gather_fusion.4
  270.6 3.2 select_multiply_fusion
  273.8 3.8 %all-to-all-start.2 = ((bf16[8,17,64,128]{3,2,1,0:T(8,128)(2,1)}), bf16[8,17,64,128]{3,2,1,0:T(8,128)(2,1)S(1)}, u32[]{:S(2)}, u32[]{:S(2)}) async-start(bf16[8,17,64,128]{3,2,1,0:T(8,128)(2,1)} %bitcast.10), calls=%async_computation.2 | async-start | bytes 4456448 | tf_op jit(solution)/shard_map/all_to_all | solution.py:94
  277.6 51.1 %all-to-all-done.2 = bf16[8,17,64,128]{3,2,1,0:T(8,128)(2,1)S(1)} async-done(((bf16[8,17,64,128]{3,2,1,0:T(8,128)(2,1)}), bf16[8,17,64,128]{3,2,1,0:T(8,128)(2,1)S(1)}, u32[]{:S(2)}, u32[]{:S(2)}) %all-to-all-start.2) | async-done | bytes 2228256 | tf_op jit(solution)/shard_map/all_to_all | solution.py:94
  328.7 2.1 gather_fusion.5
  330.9 1.9 broadcast_select_fusion
  333.2 5.3 %copy.28 = f32[4,4,64,8,128]{4,3,2,1,0:T(8,128)} copy(f32[4,4,64,8,128]{4,2,3,1,0:T(8,128)S(1)} %convert_bitcast_fusion) | data formatting | bytes 8388608 | tf_op jit(solution)/shard_map/convert_element_type | solution.py:99
  338.5 5.0 %reshape.244 = f32[4,256,1024]{2,1,0:T(8,128)} reshape(f32[4,4,64,8,128]{4,3,2,1,0:T(8,128)} %copy.28) | data formatting | bytes 8388608 | tf_op jit(solution)/shard_map/convert_element_type | solution.py:99
  343.5 6.1 %fusion.2 = bf16[4,256,1024]{2,1,0:T(8,128)(2,1)} fusion(f32[4,256,1024]{2,1,0:T(8,128)} %reshape.244, f32[4,256,1024]{2,1,0:T(8,128)} %get-tuple-element.21, bf16[4,256,1024]{2,1,0:T(8,128)(2,1)S(1)} %copy-done.3), kind=kLoop, calls=%fused_computation.10 | loop fusion | flops 4194304 | bytes 12582912 | tf_op jit(solution)/shard_map/convert_element_type | solution.py:101
  (44 shorter events, 2.5 us)
Async XLA Ops:
  6.5 11.7 %copy-start = (s32[32,16,8]{0,2,1:T(8,128)S(1)}, s32[32,16,8]{0,2,1:T(8,128)}, u32[]{:S(2)}) copy-start(s32[32,16,8]{0,2,1:T(8,128)} %param.17) | copy-start | bytes 49156
  6.5 1.6 copy-start.4
  6.5 249.4 %all-gather.2.cloned.1.call-start = ((), (), s32[]{:S(2)}) async-start(), calls=%async_computation.3 | async-start | bytes 10485760 | tf_op jit(solution)/shard_map/all_gather | solution.py:88
  12.5 144.4 %all-to-all-start = ((bf16[4,4,256,1024]{3,2,1,0:T(8,128)(2,1)}), bf16[4,4,256,1024]{3,2,1,0:T(8,128)(2,1)}, u32[]{:S(2)}, u32[]{:S(2)}) async-start(bf16[4,4,256,1024]{3,2,1,0:T(8,128)(2,1)} %stack.2), calls=%async_computation | async-start | bytes 16777216 | tf_op jit(solution)/shard_map/all_to_all | solution.py:58
  156.9 8.1 %copy-start.2 = (bf16[4,256,1024]{2,1,0:T(8,128)(2,1)S(1)}, bf16[4,256,1024]{2,1,0:T(8,128)(2,1)}, u32[]{:S(2)}) copy-start(bf16[4,256,1024]{2,1,0:T(8,128)(2,1)} %param.12) | copy-start | bytes 6291460
  156.9 8.1 %copy-start.5 = (f32[4,1024]{1,0:T(4,128)S(1)}, f32[4,1024]{1,0:T(4,128)}, u32[]{:S(2)}) copy-start(f32[4,1024]{1,0:T(4,128)} %param.14) | copy-start | bytes 49156
  179.6 57.8 %all-to-all-start.1 = ((bf16[8,17,64,128]{3,2,1,0:T(8,128)(2,1)}), bf16[8,17,64,128]{3,2,1,0:T(8,128)(2,1)S(1)}, u32[]{:S(2)}, u32[]{:S(2)}) async-start(bf16[8,17,64,128]{3,2,1,0:T(8,128)(2,1)} %bitcast.4), calls=%async_computation.1 | async-start | bytes 4456448 | tf_op jit(solution)/shard_map/all_to_all | solution.py:82
  251.0 4.9 %copy-start.6 = (f32[4,1024]{1,0:T(4,128)S(1)}, f32[4,1024]{1,0:T(4,128)}, u32[]{:S(2)}) copy-start(f32[4,1024]{1,0:T(4,128)} %param.16) | copy-start | bytes 49156
  273.8 54.9 %all-to-all-start.2 = ((bf16[8,17,64,128]{3,2,1,0:T(8,128)(2,1)}), bf16[8,17,64,128]{3,2,1,0:T(8,128)(2,1)S(1)}, u32[]{:S(2)}, u32[]{:S(2)}) async-start(bf16[8,17,64,128]{3,2,1,0:T(8,128)(2,1)} %bitcast.10), calls=%async_computation.2 | async-start | bytes 4456448 | tf_op jit(solution)/shard_map/all_to_all | solution.py:94
  338.5 5.0 %copy-start.3 = (bf16[4,256,1024]{2,1,0:T(8,128)(2,1)S(1)}, bf16[4,256,1024]{2,1,0:T(8,128)(2,1)}, u32[]{:S(2)}) copy-start(bf16[4,256,1024]{2,1,0:T(8,128)(2,1)} %param.12) | copy-start | bytes 6291460
  343.5 6.1 %copy-start.1 = (s32[32,16,8]{0,2,1:T(8,128)S(1)}, s32[32,16,8]{0,2,1:T(8,128)}, u32[]{:S(2)}) copy-start(s32[32,16,8]{0,2,1:T(8,128)} %param.17) | copy-start | bytes 49156
Sparse Core Ops, SparseCore 0:
  8.9 106.0 all-gather.1
